TPU v7x, 768 devices: a whole 4x8x12 slice. The times are simulated.
768 devices in a mesh: dp: 64 (over y, z_lo, core), tensor: 12 (over x, z_hi).
Axes of the slice: x: 4, y: 8, z: 12 (z_hi: 3, z_lo: 4; z = z_hi * 4 + z_lo), core: 2. Of those that a mesh axis runs over, the one named last changes fastest.
Arguments:
- latent: bfloat16 [36864, 512], P('dp'), may hold values from -6 to 6
- q_nope: bfloat16 [36864, 6144], P('dp', 'tensor'), may hold values from -6 to 6
- q_rope: bfloat16 [36864, 3072], P('dp', 'tensor'), may hold values from -40 to 40
- k_rope: bfloat16 [36864, 64], P('dp'), may hold values from -4.5 to 4.5
- grad_out: bfloat16 [36864, 6144], P('dp', 'tensor'), may hold values from -6 to 6
- offsets: int32 [64], P('dp'), may hold values from 1 to 575
- weight: bfloat16 [256, 48, 512], P(None, 'tensor'), may hold values from -0.25 to 0.25
- basis: float32 [512, 512], replicated, may hold values from -1 to 1
- first_moment: float32 [256, 48, 512], P('dp', 'tensor'), may hold values from -30 to 30
- second_rot: float32 [256, 48, 512], P('dp', 'tensor'), may hold values from 1 to 400
- second_plain: float32 [256, 48, 512], P('dp', 'tensor'), may hold values from 1 to 400
Outputs:
- grad_latent: bfloat16 [36864, 512], P(('dp', 'tensor'))
- new_weight: bfloat16 [256, 48, 512], P(None, 'tensor')
- new_first: float32 [256, 48, 512], P('dp', 'tensor')
- new_second: float32 [256, 48, 512], P('dp', 'tensor')
- new_plain: float32 [256, 48, 512], P('dp', 'tensor')
All inputs are finite; a program needn't handle non-finite values.
Results may differ from a plain program's by a relative error of at most 0.011.
Values may be sent and summed in bfloat16 or wider, within the bound.
A program may use at most 64 MiB of HBM per device.

v0:
```python
import jax
import jax.numpy as jnp
from jax import lax
from jax.sharding import PartitionSpec as P

beta_first = 0.9
beta_second = 0.95
epsilon = 1e-08
learn_rate = 0.002
decay_rate = 0.1
blend_share = 0.5


def in_blocks(shard, dim, peers):
    before, after = (shard.shape[:dim], shard.shape[dim + 1 :])
    return jnp.moveaxis(shard.reshape(*before, peers, -1, *after), dim, 0)


def sum_at_owner(shard, axis, dim):
    pieces = in_blocks(shard, dim, lax.axis_size(axis))
    arrived = lax.all_to_all(pieces, axis, split_axis=0, concat_axis=0, tiled=True)
    return arrived.sum(axis=0)


def sent_to_all(shard, axis):
    peers = lax.axis_size(axis)
    return lax.all_to_all(
        jnp.broadcast_to(shard[None], (peers, *shard.shape)), axis, 0, 0, tiled=True
    )


def laid_out(pieces, dim):
    shape = list(pieces.shape[1:])
    shape[dim] *= pieces.shape[0]
    return jnp.moveaxis(pieces, 0, dim).reshape(shape)


def gather_directly(shard, axis, dim):
    pieces = sent_to_all(shard, axis)
    return laid_out(pieces, dim)


def attend_back(
    query_main, query_side, key_side, key_main, value_rows, out_grads, visible, score_scale
):
    f32 = jnp.float32
    scores = (
        jnp.einsum("ihd,jhd->hij", query_main, key_main, preferred_element_type=f32)
        + jnp.einsum("ihe,je->hij", query_side, key_side, preferred_element_type=f32)
    ) * score_scale
    masked = jnp.where(visible[None], scores, -jnp.inf)
    row_max = jnp.max(masked, axis=-1, keepdims=True)
    exp_terms = jnp.where(visible[None], jnp.exp(masked - row_max), 0.0)
    attn_probs = exp_terms / jnp.sum(exp_terms, axis=-1, keepdims=True)
    probs_low = attn_probs.astype(jnp.bfloat16)
    attended = jnp.einsum("hij,jhd->ihd", probs_low, value_rows, preferred_element_type=f32)
    row_delta = jnp.sum(out_grads.astype(f32) * attended, axis=-1)
    grad_probs = jnp.einsum("ihd,jhd->hij", out_grads, value_rows, preferred_element_type=f32)
    grad_scores = (
        attn_probs * (grad_probs - jnp.transpose(row_delta)[:, :, None]) * score_scale
    ).astype(jnp.bfloat16)
    grad_keys = jnp.einsum("hij,ihd->jhd", grad_scores, query_main, preferred_element_type=f32)
    grad_values = jnp.einsum("hij,ihd->jhd", probs_low, out_grads, preferred_element_type=f32)
    return jnp.concatenate([grad_keys, grad_values], axis=-1).astype(jnp.bfloat16)


def local(
    latent,
    q_nope,
    q_rope,
    k_rope,
    grad_out,
    offsets,
    weight,
    basis,
    first_moment,
    second_rot,
    second_plain,
):
    f32 = jnp.float32
    highest = lax.Precision.HIGHEST
    seq_len = latent.shape[0]
    width_rows, head_count, latent_dim = weight.shape
    head_dim = width_rows // 2
    rope_dim = k_rope.shape[1]
    score_scale = float(head_dim + rope_dim) ** (-0.5)
    positions = jnp.arange(seq_len, dtype=jnp.int32)
    visible = positions[None, :] <= jnp.maximum(positions[:, None], offsets[0] - 1)
    query_main = q_nope.reshape(seq_len, head_count, head_dim)
    query_side = q_rope.reshape(seq_len, head_count, rope_dim)
    out_grads = grad_out.reshape(seq_len, head_count, head_dim)
    key_value = jnp.einsum("tc,rhc->thr", latent, weight, preferred_element_type=f32).astype(
        jnp.bfloat16
    )
    key_main = key_value[:, :, :head_dim]
    value_rows = key_value[:, :, head_dim:]
    slab_rows = width_rows // lax.axis_size("dp")
    grad_kv = attend_back(
        query_main, query_side, k_rope, key_main, value_rows, out_grads, visible, score_scale
    )
    slab_grad = sum_at_owner(
        jnp.einsum("thr,tc->rhc", grad_kv, latent, preferred_element_type=f32), "dp", 0
    )
    partial_value = jnp.einsum("thr,rhc->tc", grad_kv, weight, preferred_element_type=f32)
    grad_latent = sum_at_owner(partial_value, "tensor", 0).astype(jnp.bfloat16)
    own_rows = lax.dynamic_slice_in_dim(
        weight, lax.axis_index("dp") * slab_rows, slab_rows, 0
    ).astype(f32)
    rotated = jnp.einsum("rhc,ce->rhe", slab_grad, basis, precision=highest)
    moment = beta_first * first_moment + (1.0 - beta_first) * rotated
    rotated_sq = beta_second * second_rot + (1.0 - beta_second) * rotated * rotated
    plain_sq = beta_second * second_plain + (1.0 - beta_second) * slab_grad * slab_grad
    stacked = jnp.stack([moment / (jnp.sqrt(rotated_sq) + epsilon), moment])
    turned = jnp.einsum("srhe,ce->srhc", stacked, basis, precision=highest)
    direction = blend_share * turned[0] + blend_share * turned[1] / (jnp.sqrt(plain_sq) + epsilon)
    new_slab = (own_rows - learn_rate * (direction + decay_rate * own_rows)).astype(jnp.bfloat16)
    new_weight = gather_directly(new_slab, "dp", 0)
    return (grad_latent, new_weight, moment, rotated_sq, plain_sq)


def solution(mesh):
    return jax.shard_map(
        local,
        mesh=mesh,
        in_specs=(
            P("dp", None),
            P("dp", "tensor"),
            P("dp", "tensor"),
            P("dp", None),
            P("dp", "tensor"),
            P("dp"),
            P(None, "tensor", None),
            P(),
            P("dp", "tensor", None),
            P("dp", "tensor", None),
            P("dp", "tensor", None),
        ),
        out_specs=(
            P(("dp", "tensor"), None),
            P(None, "tensor", None),
            P("dp", "tensor", None),
            P("dp", "tensor", None),
            P("dp", "tensor", None),
        ),
        check_vma=False,
    )
```

profile of v0, /device:TPU:1, one launch (start us, length us, event | category | flops | bytes accessed | tf_op | source)
XLA Modules:
  0.0 198.7 jit_solution(9444539651605230265)
XLA Ops:
  0.7 1.3 copy.43
  2.8 3.3 %fusion.12 = bf16[576,4,256]{2,0,1:T(8,128)(2,1)} fusion(bf16[256,4,512]{2,1,0:T(4,128)(2,1)} %param.17, bf16[576,512]{1,0:T(8,128)(2,1)} %param.11), kind=kOutput, calls=%fused_computation.17 | convolution fusion | flops 604569600 | bytes 2818048 | tf_op jit(solution)/shard_map/tc,rhc->thr/dot_general | solution.py:92
  6.1 3.5 %fusion.45 = f32[576,576,4]{1,0,2:T(8,128)} fusion(bf16[576,4,64]{0,2,1:T(8,128)(2,1)S(1)} %bitcast.117, bf16[576,64]{0,1:T(8,128)(2,1)S(1)} %copy-done.2), kind=kOutput, calls=%fused_computation.46 | convolution fusion | flops 169869312 | bytes 5677056 | tf_op jit(solution)/shard_map/ihe,je->hij/dot_general | solution.py:49
  9.6 8.1 %fusion.67 = (f32[4,576]{1,0:T(4,128)S(1)}, f32[4,576,576]{1,2,0:T(8,128)}) fusion(pred[576,576]{0,1:T(8,128)(4,1)S(1)} %iota_compare_fusion, f32[576,576,4]{1,0,2:T(8,128)} %fusion.45, bf16[576,4,256]{2,0,1:T(8,128)(2,1)} %fusion.12, bf16[576,512]{1,0:T(8,128)(2,1)S(1)} %copy-done.6), kind=kOutput, calls=%fused_computation.75 | convolution fusion | flops 347701824 | bytes 13132800 | tf_op jit(solution)/shard_map/sub | solution.py:53
  17.8 3.3 %fusion.11 = bf16[4,576,576]{1,2,0:T(8,128)(2,1)S(1)} fusion(f32[4,576,576]{1,2,0:T(8,128)} %get-tuple-element.11, f32[4,576]{1,0:T(4,128)S(1)} %get-tuple-element.10), kind=kLoop, calls=%fused_computation.13 | loop fusion | flops 2654208 | bytes 7971840 | tf_op jit(solution)/shard_map/convert_element_type | solution.py:55
  21.1 1.3 fusion.17
  22.4 1.7 fusion.21
  24.4 5.4 %fusion.18 = bf16[576,4,128]{2,0,1:T(8,128)(2,1)} fusion(f32[4,576]{1,0:T(4,128)S(1)} %copy.48, f32[4,576,576]{1,2,0:T(8,128)} %get-tuple-element.11, f32[4,576]{1,0:T(4,128)S(1)} %get-tuple-element.10, bf16[576,4,256]{2,0,1:T(8,128)(2,1)} %fusion.12, bf16[576,512]{1,0:T(8,128)(2,1)S(1)} %copy-done.7, bf16[576,512]{1,0:T(8,128)(2,1)S(1)} %copy-done.6), kind=kOutput, calls=%fused_computation.23 | convolution fusion | flops 686407680 | bytes 8275968 | tf_op jit(solution)/shard_map/hij,ihd->jhd/dot_general | solution.py:62
  29.8 3.8 %convolution_bitcast_fusion = f32[256,4,512]{2,0,1:T(8,128)} fusion(bf16[576,4,128]{2,0,1:T(8,128)(2,1)} %fusion.21, bf16[576,4,128]{2,0,1:T(8,128)(2,1)} %fusion.18, bf16[576,512]{1,0:T(8,128)(2,1)} %param.11), kind=kOutput, calls=%fused_computation.14 | convolution fusion | flops 606339072 | bytes 3866624 | tf_op jit(solution)/shard_map/thr,tc->rhc/dot_general | solution.py:102
  33.6 1.9 reshape.66
  35.5 2.0 copy.52
  37.5 14.6 %all-to-all-start.1 = ((f32[64,4,4,512]{3,1,2,0:T(4,128)}), f32[64,4,4,512]{3,1,2,0:T(4,128)S(1)}, u32[]{:S(2)}, u32[]{:S(2)}) async-start(f32[64,4,4,512]{3,1,2,0:T(4,128)} %copy.52), calls=%async_computation.1 | async-start | bytes 4194304 | tf_op jit(solution)/shard_map/all_to_all | solution.py:21
  52.1 3.4 %fusion.26 = f32[576,512,1]{1,0,2:T(8,128)} fusion(bf16[256,4,512]{2,1,0:T(4,128)(2,1)} %param.17, bf16[576,4,128]{2,0,1:T(8,128)(2,1)} %fusion.21, bf16[576,4,128]{2,0,1:T(8,128)(2,1)} %fusion.18), kind=kOutput, calls=%fused_computation.30 | convolution fusion | flops 606339072 | bytes 3407872 | tf_op jit(solution)/shard_map/thr,rhc->tc/dot_general | solution.py:104
  55.5 45.9 %all-to-all-done.1 = f32[64,4,4,512]{3,1,2,0:T(4,128)S(1)} async-done(((f32[64,4,4,512]{3,1,2,0:T(4,128)}), f32[64,4,4,512]{3,1,2,0:T(4,128)S(1)}, u32[]{:S(2)}, u32[]{:S(2)}) %all-to-all-start.1) | async-done | bytes 2097184 | tf_op jit(solution)/shard_map/all_to_all | solution.py:21
  101.5 13.4 %all-to-all-start = ((f32[12,48,512]{2,1,0:T(8,128)}), f32[12,48,512]{2,1,0:T(8,128)}, u32[]{:S(2)}, u32[]{:S(2)}) async-start(f32[12,48,512]{2,1,0:T(8,128)} %bitcast.118), calls=%async_computation | async-start | bytes 2359296 | tf_op jit(solution)/shard_map/all_to_all | solution.py:21
  115.2 1.3 fusion.59
  116.5 1.1 fusion.22
  117.6 1.4 fusion.52
  119.0 11.3 %all-to-all-done = f32[12,48,512]{2,1,0:T(8,128)} async-done(((f32[12,48,512]{2,1,0:T(8,128)}), f32[12,48,512]{2,1,0:T(8,128)}, u32[]{:S(2)}, u32[]{:S(2)}) %all-to-all-start) | async-done | bytes 1179680 | tf_op jit(solution)/shard_map/all_to_all | solution.py:21
  130.3 1.5 broadcast_in_dim.34
  131.8 37.3 %all-to-all-start.2 = ((bf16[64,4,4,512]{3,2,1,0:T(4,128)(2,1)}), bf16[64,4,4,512]{3,2,1,0:T(4,128)(2,1)S(1)}, u32[]{:S(2)}, u32[]{:S(2)}) async-start(bf16[64,4,4,512]{3,2,1,0:T(4,128)(2,1)} %broadcast_in_dim.34), calls=%async_computation.2 | async-start | bytes 2097152 | tf_op jit(solution)/shard_map/all_to_all | solution.py:27
  169.2 2.0 reduce_sum.38
  171.2 26.6 %all-to-all-done.2 = bf16[64,4,4,512]{3,2,1,0:T(4,128)(2,1)S(1)} async-done(((bf16[64,4,4,512]{3,2,1,0:T(4,128)(2,1)}), bf16[64,4,4,512]{3,2,1,0:T(4,128)(2,1)S(1)}, u32[]{:S(2)}, u32[]{:S(2)}) %all-to-all-start.2) | async-done | bytes 1048608 | tf_op jit(solution)/shard_map/all_to_all | solution.py:27
  197.7 1.0 copy.95
  (23 shorter events, 0.9 us)
Async XLA Ops:
  0.6 114.6 %copy-start = (f32[512,512]{1,0:T(8,128)S(1)}, f32[512,512]{1,0:T(8,128)}, u32[]{:S(2)}) copy-start(f32[512,512]{1,0:T(8,128)} %param.18) | copy-start | bytes 3145732
  0.6 5.4 %copy-start.2 = (bf16[576,64]{0,1:T(8,128)(2,1)S(1)}, bf16[576,64]{0,1:T(8,128)(2,1)}, u32[]{:S(2)}) copy-start(bf16[576,64]{0,1:T(8,128)(2,1)} %param.14) | copy-start | bytes 221188
  6.1 3.5 %copy-start.6 = (bf16[576,512]{1,0:T(8,128)(2,1)S(1)}, bf16[576,512]{1,0:T(8,128)(2,1)}, u32[]{:S(2)}) copy-start(bf16[576,512]{1,0:T(8,128)(2,1)} %param.12) | copy-start | bytes 1769476
  17.8 3.3 %copy-start.7 = (bf16[576,512]{1,0:T(8,128)(2,1)S(1)}, bf16[576,512]{1,0:T(8,128)(2,1)}, u32[]{:S(2)}) copy-start(bf16[576,512]{1,0:T(8,128)(2,1)} %param.15) | copy-start | bytes 1769476
  17.8 3.3 %copy-start.8 = (bf16[576,4,256]{2,0,1:T(8,128)(2,1)S(1)}, bf16[576,4,256]{2,0,1:T(8,128)(2,1)}, u32[]{:S(2)}) copy-start(bf16[576,4,256]{2,0,1:T(8,128)(2,1)} %fusion.12) | copy-start | bytes 3538948
  37.5 64.0 %all-to-all-start.1 = ((f32[64,4,4,512]{3,1,2,0:T(4,128)}), f32[64,4,4,512]{3,1,2,0:T(4,128)S(1)}, u32[]{:S(2)}, u32[]{:S(2)}) async-start(f32[64,4,4,512]{3,1,2,0:T(4,128)} %copy.52), calls=%async_computation.1 | async-start | bytes 4194304 | tf_op jit(solution)/shard_map/all_to_all | solution.py:21
  55.5 59.7 %copy-start.3 = (f32[4,4,512]{2,1,0:T(4,128)S(1)}, f32[4,4,512]{2,1,0:T(4,128)}, u32[]{:S(2)}) copy-start(f32[4,4,512]{2,1,0:T(4,128)} %param.20) | copy-start | bytes 98308
  55.5 59.7 %copy-start.4 = (f32[4,4,512]{2,1,0:T(4,128)S(1)}, f32[4,4,512]{2,1,0:T(4,128)}, u32[]{:S(2)}) copy-start(f32[4,4,512]{2,1,0:T(4,128)} %param.19) | copy-start | bytes 98308
  101.5 28.9 %all-to-all-start = ((f32[12,48,512]{2,1,0:T(8,128)}), f32[12,48,512]{2,1,0:T(8,128)}, u32[]{:S(2)}, u32[]{:S(2)}) async-start(f32[12,48,512]{2,1,0:T(8,128)} %bitcast.118), calls=%async_computation | async-start | bytes 2359296 | tf_op jit(solution)/shard_map/all_to_all | solution.py:21
  114.8 2.8 %copy-start.5 = (f32[4,4,512]{2,1,0:T(4,128)S(1)}, f32[4,4,512]{2,1,0:T(4,128)}, u32[]{:S(2)}) copy-start(f32[4,4,512]{2,1,0:T(4,128)} %param.21) | copy-start | bytes 98308
  116.5 54.6 %copy-start.1 = (f32[4,4,512]{2,1,0:T(4,128)}, f32[4,4,512]{2,1,0:T(4,128)S(1)}, u32[]{:S(2)}) copy-start(f32[4,4,512]{2,1,0:T(4,128)S(1)} %get-tuple-element.19) | copy-start | bytes 98308
  131.8 65.9 %all-to-all-start.2 = ((bf16[64,4,4,512]{3,2,1,0:T(4,128)(2,1)}), bf16[64,4,4,512]{3,2,1,0:T(4,128)(2,1)S(1)}, u32[]{:S(2)}, u32[]{:S(2)}) async-start(bf16[64,4,4,512]{3,2,1,0:T(4,128)(2,1)} %broadcast_in_dim.34), calls=%async_computation.2 | async-start | bytes 2097152 | tf_op jit(solution)/shard_map/all_to_all | solution.py:27
where the time goes:
time: 199 us
  waiting for transfers between devices  83.8 us (42%)
  starting transfers between devices  65.3 us (33%)
  matrix products  33 us (17%)
  local copies, waits for them, and re-layouts  7.88 us (4%)
  other arithmetic  7.24 us (4%)
    all_to_all x2, waiting for transfers between devices, sum_at_owner(): lax.all_to_all(pieces, axis, split_axis=0, concat_axis=0, tiled=True)  57.3 us
    all_to_all x1, starting transfers between devices, sent_to_all(): lax.all_to_all(jnp.broadcast_to(shard[None], (peers, *shard.shape)), axis...  37.3 us
    all_to_all x2, starting transfers between devices, sum_at_owner(): lax.all_to_all(pieces, axis, split_axis=0, concat_axis=0, tiled=True)  28 us
    all_to_all x1, waiting for transfers between devices, sent_to_all(): lax.all_to_all(jnp.broadcast_to(shard[None], (peers, *shard.shape)), axis...  26.6 us
    sub x1, matrix products, attend_back(): exp_terms = jnp.where(visible[None], jnp.exp(masked - row_max), 0.0)  8.15 us
    dot_general x1, matrix products, attend_back(): jnp.einsum('hij,ihd->jhd', grad_scores, query_main, preferred_element_typ...  5.45 us
  transfers between devices with their start and end apart: 3, of which 3 were waited for; matrix products, arithmetic and copies ran while one was open for 5% of the time, Pallas kernels for 0%

commit v1 on v0

v1 whole, which is shorter than its diff:
```python
import functools
import math

import jax
import jax.numpy as jnp
from jax import lax
from jax.experimental import pallas as pl
from jax.experimental.pallas import tpu as pltpu
from jax.sharding import PartitionSpec as P

beta_first = 0.9
beta_second = 0.95
epsilon = 1e-08
learn_rate = 0.002
decay_rate = 0.1
blend_share = 0.5

NY, NZ, NC = 8, 4, 2
NX, NH = 4, 3
f32 = jnp.float32
bf16 = jnp.bfloat16

NN = (((1,), (0,)), ((), ()))
NT = (((1,), (1,)), ((), ()))


def mm(a, b, dims=NN):
    return lax.dot_general(a, b, dims, preferred_element_type=f32)


def iota(shape, dim):
    return lax.broadcasted_iota(jnp.int32, shape, dim)


def one_hot_rows(source, columns):
    return jnp.where(source == iota((source.shape[0], columns), 1), 1.0, 0.0).astype(bf16)


def split(x):
    high = x.astype(bf16)
    return high, (x - high.astype(f32)).astype(bf16)


def kernel(
    off, lat, qn, qr, kr, go, w, basis, fm, sr, sp,
    gl_out, gw, nf_out, ns_out, np_out,
    krp, gkv, pts, gss, wg_own, wg_send, c_recv, y_send, y_recv, zsrc, z_send, z_recv,
    gl_send, x_recv, zh_send, zh_recv, b_hi, b_lo, t_fm, t_sr, t_sp,
    c_ss, c_rs, y_ss, y_rs, z_ss, z_rs, x_ss, x_rs, h_ss, h_rs,
    a1_ss, a1_rs, b1_ss, b1_rs, a2_ss, a2_rs, b2_ss, b2_rs, ga_ss, ga_rs, gb_ss, gb_rs,
):
    seq, _ = lat.shape
    heads, rows, latw = w.shape
    hd = rows // 2
    half = latw // 2
    dp = lax.axis_index("dp")
    tn = lax.axis_index("tensor")
    my_y, my_z, my_c = dp // (NZ * NC), (dp // NC) % NZ, dp % NC
    my_x, my_h = tn // NH, tn % NH

    def at_y(k):
        return (((my_y + k) % NY) * (NZ * NC) + my_z * NC + my_c, tn)

    def at_z(k):
        return (my_y * (NZ * NC) + ((my_z + k) % NZ) * NC + my_c, tn)

    def at_x(k):
        return (dp, ((my_x + k) % NX) * NH + my_h)

    def at_h(k):
        return (dp, my_x * NH + (my_h + k) % NH)

    partner = (my_y * (NZ * NC) + my_z * NC + (1 - my_c), tn)

    def remote(src, dst, ss, rs, to):
        return pltpu.make_async_remote_copy(
            src_ref=src, dst_ref=dst, send_sem=ss, recv_sem=rs,
            device_id=to, device_id_type=pl.DeviceIdType.MESH,
        )

    barrier = pltpu.get_barrier_semaphore()
    greet = (
        [partner]
        + [at_y(k) for k in range(1, NY)]
        + [at_z(k) for k in range(1, NZ)]
        + [at_x(k) for k in range(1, NX)]
        + [at_h(k) for k in range(1, NH)]
    )
    for to in greet:
        pl.semaphore_signal(barrier, inc=1, device_id=to, device_id_type=pl.DeviceIdType.MESH)

    sent = []

    lane = iota((kr.shape[1], 2 * kr.shape[1]), 1)
    row = iota((kr.shape[1], 2 * kr.shape[1]), 0)
    for odd in range(2):
        place = jnp.where(lane == row + odd * kr.shape[1], 1.0, 0.0).astype(bf16)
        krp[odd] = mm(kr[...], place).astype(bf16)

    o = iota((rows, 1), 0)
    src_row = (
        ((o >> 4) & 7) * 32 + ((o >> 2) & 3) * 8 + jnp.where((o >> 7) == 0, my_c, 1 - my_c) * 4 + (o & 3)
    )
    perm = one_hot_rows(src_row, rows)

    scale = float(hd + kr.shape[1]) ** (-0.5)
    to_exp2 = scale * math.log2(math.e)
    last_seen = off[0] - 1
    blocks = [(0, 256), (256, 256), (512, seq - 512)]

    def core_copy(h):
        return remote(wg_send.at[h], c_recv.at[h], c_ss.at[h], c_rs.at[h], partner)

    def y_copy(h, k):
        return remote(
            y_send.at[h, (my_y + k) % NY], y_recv.at[h, k - 1],
            y_ss.at[h, k - 1], y_rs.at[h, k - 1], at_y(k),
        )

    def finish_core(h):
        copy = core_copy(h)
        copy.wait_recv()
        both = wg_own[h] + c_recv[h].astype(f32)
        y_send[h] = both.astype(bf16).reshape(NY, rows // 16, latw)
        for k in (4, 3, 5, 2, 6, 1, 7):
            c = y_copy(h, k)
            c.start()
            sent.append(c)

    for h in range(heads):
        lanes = slice(h * hd, (h + 1) * hd)
        pair = slice((h // 2) * hd, (h // 2 + 1) * hd)
        kv = mm(lat[...], w[h], NT).astype(bf16)
        key = jnp.concatenate([kv[:, :hd], krp[h % 2]], axis=1)
        value = kv[:, hd:]
        buf = h % 2
        for start, size in blocks:
            at = slice(start, start + size)
            query = jnp.concatenate([qn[at, lanes], qr[at, pair]], axis=1)
            scores = mm(key, query, NT)
            limit = jnp.maximum(iota((1, size), 1) + start, last_seen)
            seen = iota((seq, size), 0) <= limit
            masked = jnp.where(seen, scores, -jnp.inf)
            top = jnp.max(masked, axis=0, keepdims=True)
            terms = jnp.exp2((masked - top) * to_exp2)
            probs = terms * (1.0 / jnp.sum(terms, axis=0, keepdims=True))
            low = probs.astype(bf16)
            pts[buf, :, at] = low
            grad_probs = mm(value, go[at, lanes], NT)
            delta = jnp.sum(low.astype(f32) * grad_probs, axis=0, keepdims=True)
            gss[buf, :, at] = (probs * (grad_probs - delta) * scale).astype(bf16)
        grad_keys = mm(gss[buf], qn[:, lanes])
        grad_values = mm(pts[buf], go[:, lanes])
        both = jnp.concatenate([grad_keys.astype(bf16), grad_values.astype(bf16)], axis=1)
        gkv[h] = both
        turned = mm(perm, both, NT).astype(bf16)
        part = mm(turned, lat[...])
        wg_own[h] = part[: rows // 2]
        wg_send[h] = part[rows // 2 :].astype(bf16)
        if h == 0:
            pl.semaphore_wait(barrier, len(greet))
        c = core_copy(h)
        c.start()
        sent.append(c)
        if h > 0:
            finish_core(h - 1)

    share = seq // NX
    for xb in range(NX):
        at = slice(xb * share, (xb + 1) * share)
        total = mm(gkv[0, at], w[0])
        for h in range(1, heads):
            total = total + mm(gkv[h, at], w[h])
        gl_send[xb] = total.astype(bf16)

    finish_core(heads - 1)

    def x_copy(k):
        return remote(
            gl_send.at[(my_x + k) % NX], x_recv.at[k - 1], x_ss.at[k - 1], x_rs.at[k - 1], at_x(k)
        )

    for k in (2, 1, 3):
        c = x_copy(k)
        c.start()
        sent.append(c)

    high, low = split(basis[...])
    b_hi[...] = high
    b_lo[...] = low
    per = rows // (NY * NZ * NC)
    for i in range(per):
        at = slice(i * heads, (i + 1) * heads)
        t_fm[at] = fm[i]
        t_sr[at] = sr[i]
        t_sp[at] = sp[i]
    near = pl.multiple_of((dp // 4) * 16, 16)
    o = iota((16, 1), 0)
    old = jnp.zeros((16, latw), f32)
    for h in range(heads):
        pick = jnp.where((o & 3) == h, (dp % 4) * 4 + (o >> 2), -1)
        old = old + mm(one_hot_rows(pick, 16), w[h, pl.ds(near, 16), :])

    for h in range(heads):
        total = y_send[h, my_y].astype(f32)
        for k in range(1, NY):
            y_copy(h, k).wait_recv()
            total = total + y_recv[h, k - 1].astype(f32)
        zsrc[h * 16 : (h + 1) * 16] = total.astype(bf16)
    o = iota((heads * 16, 1), 0)
    order = one_hot_rows((o & 3) * 16 + (o >> 4) * 4 + ((o >> 2) & 3), heads * 16)
    z_send[...] = mm(order, zsrc[...]).astype(bf16).reshape(NZ, 16, latw)

    def z_copy(k):
        return remote(
            z_send.at[(my_z + k) % NZ], z_recv.at[k - 1], z_ss.at[k - 1], z_rs.at[k - 1], at_z(k)
        )

    for k in range(1, NZ):
        c = z_copy(k)
        c.start()
        sent.append(c)

    total = gl_send[my_x].astype(f32)
    for k in range(1, NX):
        x_copy(k).wait_recv()
        total = total + x_recv[k - 1].astype(f32)
    zh_send[...] = total.astype(bf16).reshape(NH, share // NH, latw)

    def h_copy(k):
        return remote(
            zh_send.at[(my_h + k) % NH], zh_recv.at[k - 1], h_ss.at[k - 1], h_rs.at[k - 1], at_h(k)
        )

    for k in range(1, NH):
        c = h_copy(k)
        c.start()
        sent.append(c)

    grad = z_send[my_z].astype(f32)
    for k in range(1, NZ):
        z_copy(k).wait_recv()
        grad = grad + z_recv[k - 1].astype(f32)

    g_hi, g_lo = split(grad)
    rotated = mm(g_hi, b_hi[...]) + mm(g_lo, b_hi[...]) + mm(g_hi, b_lo[...])
    first = beta_first * t_fm[...] + (1.0 - beta_first) * rotated
    second = beta_second * t_sr[...] + (1.0 - beta_second) * rotated * rotated
    plain = beta_second * t_sp[...] + (1.0 - beta_second) * grad * grad
    stacked = jnp.concatenate([first / (jnp.sqrt(second) + epsilon), first], axis=0)
    s_hi, s_lo = split(stacked)
    back = mm(s_hi, b_hi[...], NT) + mm(s_lo, b_hi[...], NT) + mm(s_hi, b_lo[...], NT)
    direction = blend_share * back[:16] + blend_share * back[16:] / (jnp.sqrt(plain) + epsilon)
    new = (old - learn_rate * (direction + decay_rate * old)).astype(bf16)
    gw[my_y, my_z, my_c] = new

    lo, hi = slice(0, half), slice(half, latw)

    def a1(k):
        ref = gw.at[my_y, my_z, my_c, :, lo]
        return remote(ref, ref, a1_ss.at[k - 1], a1_rs.at[k - 1], at_z(k))

    def b1(k):
        ref = gw.at[my_y, my_z, my_c, :, hi]
        return remote(ref, ref, b1_ss.at[k - 1], b1_rs.at[k - 1], at_y(k))

    def a2(k):
        ref = gw.at[my_y, :, my_c, :, lo]
        return remote(ref, ref, a2_ss.at[k - 1], a2_rs.at[k - 1], at_y(k))

    def b2(k):
        ref = gw.at[:, my_z, my_c, :, hi]
        return remote(ref, ref, b2_ss.at[k - 1], b2_rs.at[k - 1], at_z(k))

    def ga(k):
        ref = gw.at[(my_y + NY - k) % NY, :, my_c, :, lo]
        return remote(ref, ref, ga_ss.at[k], ga_rs.at[k], partner)

    def gb(k):
        ref = gw.at[:, (my_z + NZ - k) % NZ, my_c, :, hi]
        return remote(ref, ref, gb_ss.at[k], gb_rs.at[k], partner)

    def go_on(c):
        c.start()
        sent.append(c)

    for k in (1, 2, 3):
        go_on(a1(k))
    for k in (4, 3, 5, 2, 6, 1, 7):
        go_on(b1(k))

    for i in range(per):
        at = slice(i * heads, (i + 1) * heads)
        nf_out[i] = first[at]
        ns_out[i] = second[at]
        np_out[i] = plain[at]

    for k in (1, 2, 3):
        a1(k).wait_recv()
    for k in (4, 3, 5, 2, 6, 1, 7):
        go_on(a2(k))
    for k in range(1, NY):
        b1(k).wait_recv()
    for k in (3, 2, 1):
        go_on(b2(k))
    go_on(ga(0))
    go_on(gb(0))

    total = zh_send[my_h].astype(f32)
    for k in range(1, NH):
        h_copy(k).wait_recv()
        total = total + zh_recv[k - 1].astype(f32)
    gl_out[...] = total.astype(bf16)

    for k in (1, 7, 2, 6, 3, 5, 4):
        a2(k).wait_recv()
        go_on(ga(k))
    for k in (1, 2, 3):
        b2(k).wait_recv()
        go_on(gb(k))
    for k in range(NY):
        ga(k).wait_recv()
    for k in range(NZ):
        gb(k).wait_recv()
    for c in sent:
        c.wait_send()


def local(
    latent, q_nope, q_rope, k_rope, grad_out, offsets, weight, basis,
    first_moment, second_rot, second_plain,
):
    seq, latw = latent.shape
    rows, heads, _ = weight.shape
    per = first_moment.shape[0]
    by_head = jnp.transpose(weight, (1, 0, 2))
    vmem = pl.BlockSpec(memory_space=pltpu.VMEM)
    dma = pltpu.SemaphoreType.DMA
    V = pltpu.VMEM
    share = seq // NX
    outs = pl.pallas_call(
        kernel,
        out_shape=(
            jax.ShapeDtypeStruct((share // NH, latw), bf16),
            jax.ShapeDtypeStruct((NY, NZ, NC, per * heads, latw), bf16),
            jax.ShapeDtypeStruct((per, heads, latw), f32),
            jax.ShapeDtypeStruct((per, heads, latw), f32),
            jax.ShapeDtypeStruct((per, heads, latw), f32),
        ),
        in_specs=[pl.BlockSpec(memory_space=pltpu.SMEM)] + [vmem] * 10,
        out_specs=[vmem] * 5,
        scratch_shapes=[
            V((2, seq, 128), bf16),
            V((heads, seq, rows), bf16),
            V((2, seq, seq), bf16),
            V((2, seq, seq), bf16),
            V((heads, rows // 2, latw), f32),
            V((heads, rows // 2, latw), bf16),
            V((heads, rows // 2, latw), bf16),
            V((heads, NY, 16, latw), bf16),
            V((heads, NY - 1, 16, latw), bf16),
            V((heads * 16, latw), bf16),
            V((NZ, 16, latw), bf16),
            V((NZ - 1, 16, latw), bf16),
            V((NX, share, latw), bf16),
            V((NX - 1, share, latw), bf16),
            V((NH, share // NH, latw), bf16),
            V((NH - 1, share // NH, latw), bf16),
            V((latw, latw), bf16),
            V((latw, latw), bf16),
            V((16, latw), f32),
            V((16, latw), f32),
            V((16, latw), f32),
            dma((heads,)), dma((heads,)),
            dma((heads, NY - 1)), dma((heads, NY - 1)),
            dma((NZ - 1,)), dma((NZ - 1,)),
            dma((NX - 1,)), dma((NX - 1,)),
            dma((NH - 1,)), dma((NH - 1,)),
            dma((NZ - 1,)), dma((NZ - 1,)),
            dma((NY - 1,)), dma((NY - 1,)),
            dma((NY - 1,)), dma((NY - 1,)),
            dma((NZ - 1,)), dma((NZ - 1,)),
            dma((NY,)), dma((NY,)),
            dma((NZ,)), dma((NZ,)),
        ],
        compiler_params=pltpu.CompilerParams(
            collective_id=0, has_side_effects=True, vmem_limit_bytes=60 * 2**20
        ),
    )(
        offsets, latent, q_nope, q_rope, k_rope, grad_out, by_head, basis,
        first_moment, second_rot, second_plain,
    )
    grad_latent, gathered, moment, rotated_sq, plain_sq = outs
    return (grad_latent, gathered.reshape(rows, heads, latw), moment, rotated_sq, plain_sq)


def solution(mesh):
    return jax.shard_map(
        local,
        mesh=mesh,
        in_specs=(
            P("dp", None),
            P("dp", "tensor"),
            P("dp", "tensor"),
            P("dp", None),
            P("dp", "tensor"),
            P("dp"),
            P(None, "tensor", None),
            P(),
            P("dp", "tensor", None),
            P("dp", "tensor", None),
            P("dp", "tensor", None),
        ),
        out_specs=(
            P(("dp", "tensor"), None),
            P(None, "tensor", None),
            P("dp", "tensor", None),
            P("dp", "tensor", None),
            P("dp", "tensor", None),
        ),
        check_vma=False,
    )
```

time: 199 us -> 69.9 us (0.35)
  waiting for transfers between devices: 83.8 us -> 0 us
  starting transfers between devices: 65.3 us -> 0 us
  Pallas kernels: 0 us -> 59.1 us
  matrix products: 33 us -> 0 us
  other arithmetic: 7.24 us -> 0 us
    all_to_all x3 -> x0, waiting for transfers between devices: 83.8 us -> none  [the longest x2 57.3 us: sum_at_owner(): lax.all_to_all(pieces, axis, split_axis=0, concat_axis=0, tiled=True)]
    all_to_all x3 -> x0, starting transfers between devices: 65.3 us -> none  [the longest x1 37.3 us: sent_to_all(): lax.all_to_all(jnp.broadcast_to(shard[None], (peers, *shard.shape)), axis...]
    pallas_call x0 -> x1, Pallas kernels: none -> 59.1 us  [local(): pl.pallas_call(kernel, out_shape=(jax.ShapeDtypeStruct((share // NH, latw...]
    dot_general x9 -> x0, matrix products: 24.8 us -> none  [the longest x1 5.45 us: attend_back(): jnp.einsum('hij,ihd->jhd', grad_scores, query_main, preferred_element_typ...]
    sub x1 -> x0, matrix products: 8.15 us -> none  [attend_back(): exp_terms = jnp.where(visible[None], jnp.exp(masked - row_max), 0.0)]
    convert_element_type x2 -> x0, other arithmetic: 4.65 us -> none  [the longest x1 3.27 us: attend_back(): probs_low = attn_probs.astype(jnp.bfloat16)]
    unnamed x21 -> x14, local copies, waits for them, and re-layouts: 2.43 us -> 6.96 us
    reduce_sum x2 -> x0, other arithmetic: 2.35 us -> none  [sum_at_owner(): return arrived.sum(axis=0)]
  transfers between devices with their start and end apart: 3 -> 0, of which waited for: 3 -> 0; matrix products, arithmetic and copies ran while one was open for 5% -> 0% of each run, Pallas kernels for 0% -> 0%
where the time goes in v1:
time: 69.9 us; the launch traced here: 69.5 us
  Pallas kernels  59.1 us (85%)
  local copies, waits for them, and re-layouts  9.11 us (13%)
  between operations  1.3 us (2%)
    pallas_call x1, Pallas kernels, local(): pl.pallas_call(kernel, out_shape=(jax.ShapeDtypeStruct((share // NH, latw...  59.1 us
    unnamed x14, local copies, waits for them, and re-layouts  6.96 us
    reshape x1, local copies, waits for them, and re-layouts, local(): gathered.reshape(rows, heads, latw)  2.15 us

profile of v1, /device:TPU:1, one launch (start us, length us, event | category | flops | bytes accessed | tf_op | source)
XLA Modules:
  0.0 69.5 jit_solution(11031677776870394727)
XLA Ops:
  1.3 1.7 %copy.17.kr = bf16[576,64]{1,0:T(8,128)(2,1)} copy(bf16[576,64]{0,1:T(8,128)(2,1)} %param.14) | data formatting | bytes 147456 | tf_op args[3]
  2.9 2.4 %copy.19 = bf16[256,4,512]{2,0,1:T(8,128)(2,1)} copy(bf16[256,4,512]{2,1,0:T(4,128)(2,1)} %param.17) | data formatting | bytes 2097152 | tf_op args[6]
  5.3 59.1 %shard_map.146 = (bf16[48,512]{1,0:T(8,128)(2,1)}, bf16[8,4,2,16,512]{4,3,2,1,0:T(8,128)(2,1)}, f32[4,4,512]{2,1,0:T(4,128)}, f32[4,4,512]{2,1,0:T(4,128)}, f32[4,4,512]{2,1,0:T(4,128)}) custom-call(s32[1]{0:T(128)S(6)} %copy.24.off, bf16[576,512]{1,0:T(8,128)(2,1)} %lat.1, bf16[576,512]{1,0:T(8,128)(2,1)} %qn.1, bf16[576,256]{1,0:T(8,128)(2,1)} %qr.1, ...), custom_call_target="tpu_custom_call" | custom-call | tf_op jit(solution)/shard_map/pallas_call | solution.py:341
  64.4 0.0 copy-start
  64.4 2.1 %reshape.13 = bf16[256,4,512]{2,1,0:T(4,128)(2,1)} reshape(bf16[8,4,2,16,512]{4,3,2,1,0:T(8,128)(2,1)} %get-tuple-element.11) | data formatting | bytes 2097152 | tf_op jit(solution)/shard_map/reshape | solution.py:394
  66.6 0.0 copy-done
  66.6 0.0 copy-start.3
  66.6 0.6 copy.25
  67.2 0.1 copy-done.3
  67.3 0.0 copy-start.2
  67.3 0.6 copy.26
  67.9 0.2 copy-done.2
  68.1 0.0 copy-start.1
  68.1 0.6 copy.27
  68.7 0.2 copy-done.1
  68.9 0.6 copy.28
Async XLA Ops:
  64.4 2.2 %copy-start = (bf16[48,512]{1,0:T(8,128)(2,1)S(1)}, bf16[48,512]{1,0:T(8,128)(2,1)}, u32[]{:S(2)}) copy-start(bf16[48,512]{1,0:T(8,128)(2,1)} %get-tuple-element.20) | copy-start | bytes 147460
  66.6 0.8 %copy-start.3 = (f32[4,4,512]{2,1,0:T(4,128)S(1)}, f32[4,4,512]{2,1,0:T(4,128)}, u32[]{:S(2)}) copy-start(f32[4,4,512]{2,1,0:T(4,128)} %get-tuple-element.22) | copy-start | bytes 98308
  67.3 0.8 %copy-start.2 = (f32[4,4,512]{2,1,0:T(4,128)S(1)}, f32[4,4,512]{2,1,0:T(4,128)}, u32[]{:S(2)}) copy-start(f32[4,4,512]{2,1,0:T(4,128)} %get-tuple-element.23) | copy-start | bytes 98308
  68.1 0.8 %copy-start.1 = (f32[4,4,512]{2,1,0:T(4,128)S(1)}, f32[4,4,512]{2,1,0:T(4,128)}, u32[]{:S(2)}) copy-start(f32[4,4,512]{2,1,0:T(4,128)} %get-tuple-element.24) | copy-start | bytes 98308

commit v2 on v1

--- a/solution.py
+++ b/solution.py
@@ -22,6 +22,7 @@
 
 NN = (((1,), (0,)), ((), ()))
 NT = (((1,), (1,)), ((), ()))
+TN = (((0,), (0,)), ((), ()))
 
 
 def mm(a, b, dims=NN):
@@ -44,9 +45,10 @@
 def kernel(
     off, lat, qn, qr, kr, go, w, basis, fm, sr, sp,
     gl_out, gw, nf_out, ns_out, np_out,
-    krp, gkv, pts, gss, wg_own, wg_send, c_recv, y_send, y_recv, zsrc, z_send, z_recv,
+    krp, gkv, pts, gss, wg_own, wg_send, c_recv, y_send, y_recv, z_send, z_recv,
+    asrc, bsrc, za_send, za_recv, yb_send, yb_recv,
     gl_send, x_recv, zh_send, zh_recv, b_hi, b_lo, t_fm, t_sr, t_sp,
-    c_ss, c_rs, y_ss, y_rs, z_ss, z_rs, x_ss, x_rs, h_ss, h_rs,
+    c_ss, c_rs, y_ss, y_rs, z_ss, z_rs, za_ss, za_rs, yb_ss, yb_rs, x_ss, x_rs, h_ss, h_rs,
     a1_ss, a1_rs, b1_ss, b1_rs, a2_ss, a2_rs, b2_ss, b2_rs, ga_ss, ga_rs, gb_ss, gb_rs,
 ):
     seq, _ = lat.shape
@@ -91,19 +93,19 @@
 
     sent = []
 
-    lane = iota((kr.shape[1], 2 * kr.shape[1]), 1)
-    row = iota((kr.shape[1], 2 * kr.shape[1]), 0)
+    rope = kr.shape[0]
+    lane = iota((rope, 2 * rope), 1)
+    row = iota((rope, 2 * rope), 0)
     for odd in range(2):
-        place = jnp.where(lane == row + odd * kr.shape[1], 1.0, 0.0).astype(bf16)
-        krp[odd] = mm(kr[...], place).astype(bf16)
+        place = jnp.where(lane == row + odd * rope, 1.0, 0.0).astype(bf16)
+        krp[odd] = mm(kr[...], place, TN).astype(bf16)
 
     o = iota((rows, 1), 0)
-    src_row = (
-        ((o >> 4) & 7) * 32 + ((o >> 2) & 3) * 8 + jnp.where((o >> 7) == 0, my_c, 1 - my_c) * 4 + (o & 3)
-    )
-    perm = one_hot_rows(src_row, rows)
-
-    scale = float(hd + kr.shape[1]) ** (-0.5)
+    core_i = jnp.where((o >> 7) == 0, my_c, 1 - my_c) * 4 + (o & 3)
+    perm_a = one_hot_rows(((o >> 4) & 7) * 32 + ((o >> 2) & 3) * 8 + core_i, rows)
+    perm_b = one_hot_rows(((o >> 2) & 7) * 32 + ((o >> 5) & 3) * 8 + core_i, rows)
+
+    scale = float(hd + rope) ** (-0.5)
     to_exp2 = scale * math.log2(math.e)
     last_seen = off[0] - 1
     blocks = [(0, 256), (256, 256), (512, seq - 512)]
@@ -117,15 +119,26 @@
             y_ss.at[h, k - 1], y_rs.at[h, k - 1], at_y(k),
         )
 
+    def z_copy(h, k):
+        return remote(
+            z_send.at[h, (my_z + k) % NZ], z_recv.at[h, k - 1],
+            z_ss.at[h, k - 1], z_rs.at[h, k - 1], at_z(k),
+        )
+
+    def go_on(c):
+        c.start()
+        sent.append(c)
+
     def finish_core(h):
-        copy = core_copy(h)
-        copy.wait_recv()
-        both = wg_own[h] + c_recv[h].astype(f32)
-        y_send[h] = both.astype(bf16).reshape(NY, rows // 16, latw)
+        core_copy(h).wait_recv()
+        both = (wg_own[h, 0] + c_recv[h, 0].astype(f32)).astype(bf16)
+        y_send[h] = both.reshape(NY, 16, half)
+        both = (wg_own[h, 1] + c_recv[h, 1].astype(f32)).astype(bf16)
+        z_send[h] = both.reshape(NZ, 32, half)
         for k in (4, 3, 5, 2, 6, 1, 7):
-            c = y_copy(h, k)
-            c.start()
-            sent.append(c)
+            go_on(y_copy(h, k))
+        for k in (2, 1, 3):
+            go_on(z_copy(h, k))
 
     for h in range(heads):
         lanes = slice(h * hd, (h + 1) * hd)
@@ -153,10 +166,11 @@
         grad_values = mm(pts[buf], go[:, lanes])
         both = jnp.concatenate([grad_keys.astype(bf16), grad_values.astype(bf16)], axis=1)
         gkv[h] = both
-        turned = mm(perm, both, NT).astype(bf16)
-        part = mm(turned, lat[...])
-        wg_own[h] = part[: rows // 2]
-        wg_send[h] = part[rows // 2 :].astype(bf16)
+        for side, perm in ((0, perm_a), (1, perm_b)):
+            turned = mm(perm, both, NT).astype(bf16)
+            part = mm(turned, lat[:, side * half : (side + 1) * half])
+            wg_own[h, side] = part[: rows // 2]
+            wg_send[h, side] = part[rows // 2 :].astype(bf16)
         if h == 0:
             pl.semaphore_wait(barrier, len(greet))
         c = core_copy(h)
@@ -202,24 +216,40 @@
         old = old + mm(one_hot_rows(pick, 16), w[h, pl.ds(near, 16), :])
 
     for h in range(heads):
+        total = z_send[h, my_z].astype(f32)
+        for k in range(1, NZ):
+            z_copy(h, k).wait_recv()
+            total = total + z_recv[h, k - 1].astype(f32)
+        bsrc[h * 32 : (h + 1) * 32] = total.astype(bf16)
+    o = iota((heads * 32, 1), 0)
+    order = one_hot_rows((o & 3) * 32 + (o >> 4) * 4 + ((o >> 2) & 3), heads * 32)
+    yb_send[...] = mm(order, bsrc[...]).astype(bf16).reshape(NY, 16, half)
+
+    def yb_copy(k):
+        return remote(
+            yb_send.at[(my_y + k) % NY], yb_recv.at[k - 1], yb_ss.at[k - 1], yb_rs.at[k - 1], at_y(k)
+        )
+
+    for k in (4, 3, 5, 2, 6, 1, 7):
+        go_on(yb_copy(k))
+
+    for h in range(heads):
         total = y_send[h, my_y].astype(f32)
         for k in range(1, NY):
             y_copy(h, k).wait_recv()
             total = total + y_recv[h, k - 1].astype(f32)
-        zsrc[h * 16 : (h + 1) * 16] = total.astype(bf16)
+        asrc[h * 16 : (h + 1) * 16] = total.astype(bf16)
     o = iota((heads * 16, 1), 0)
     order = one_hot_rows((o & 3) * 16 + (o >> 4) * 4 + ((o >> 2) & 3), heads * 16)
-    z_send[...] = mm(order, zsrc[...]).astype(bf16).reshape(NZ, 16, latw)
-
-    def z_copy(k):
-        return remote(
-            z_send.at[(my_z + k) % NZ], z_recv.at[k - 1], z_ss.at[k - 1], z_rs.at[k - 1], at_z(k)
-        )
-
-    for k in range(1, NZ):
-        c = z_copy(k)
-        c.start()
-        sent.append(c)
+    za_send[...] = mm(order, asrc[...]).astype(bf16).reshape(NZ, 16, half)
+
+    def za_copy(k):
+        return remote(
+            za_send.at[(my_z + k) % NZ], za_recv.at[k - 1], za_ss.at[k - 1], za_rs.at[k - 1], at_z(k)
+        )
+
+    for k in (2, 1, 3):
+        go_on(za_copy(k))
 
     total = gl_send[my_x].astype(f32)
     for k in range(1, NX):
@@ -237,10 +267,15 @@
         c.start()
         sent.append(c)
 
-    grad = z_send[my_z].astype(f32)
+    lower = za_send[my_z].astype(f32)
     for k in range(1, NZ):
-        z_copy(k).wait_recv()
-        grad = grad + z_recv[k - 1].astype(f32)
+        za_copy(k).wait_recv()
+        lower = lower + za_recv[k - 1].astype(f32)
+    upper = yb_send[my_y].astype(f32)
+    for k in range(1, NY):
+        yb_copy(k).wait_recv()
+        upper = upper + yb_recv[k - 1].astype(f32)
+    grad = jnp.concatenate([lower, upper], axis=1)
 
     g_hi, g_lo = split(grad)
     rotated = mm(g_hi, b_hi[...]) + mm(g_lo, b_hi[...]) + mm(g_hi, b_lo[...])
@@ -252,42 +287,51 @@
     back = mm(s_hi, b_hi[...], NT) + mm(s_lo, b_hi[...], NT) + mm(s_hi, b_lo[...], NT)
     direction = blend_share * back[:16] + blend_share * back[16:] / (jnp.sqrt(plain) + epsilon)
     new = (old - learn_rate * (direction + decay_rate * old)).astype(bf16)
-    gw[my_y, my_z, my_c] = new
-
-    lo, hi = slice(0, half), slice(half, latw)
+    for i in range(per):
+        gw[my_y, my_z, my_c, i] = new[i * heads : (i + 1) * heads]
+
+    lo, hi = slice(0, per // 2), slice(per // 2, per)
+
+    def y_of(j):
+        return (my_y + NY - j) % NY
+
+    def z_of(j):
+        return (my_z + NZ - j) % NZ
 
     def a1(k):
-        ref = gw.at[my_y, my_z, my_c, :, lo]
+        ref = gw.at[my_y, my_z, my_c, lo]
         return remote(ref, ref, a1_ss.at[k - 1], a1_rs.at[k - 1], at_z(k))
 
     def b1(k):
-        ref = gw.at[my_y, my_z, my_c, :, hi]
+        ref = gw.at[my_y, my_z, my_c, hi]
         return remote(ref, ref, b1_ss.at[k - 1], b1_rs.at[k - 1], at_y(k))
 
-    def a2(k):
-        ref = gw.at[my_y, :, my_c, :, lo]
-        return remote(ref, ref, a2_ss.at[k - 1], a2_rs.at[k - 1], at_y(k))
-
-    def b2(k):
-        ref = gw.at[:, my_z, my_c, :, hi]
-        return remote(ref, ref, b2_ss.at[k - 1], b2_rs.at[k - 1], at_z(k))
+    def a2(j, k):
+        ref = gw.at[my_y, z_of(j), my_c, lo]
+        return remote(ref, ref, a2_ss.at[j, k - 1], a2_rs.at[j, k - 1], at_y(k))
+
+    def b2(j, k):
+        ref = gw.at[y_of(j), my_z, my_c, hi]
+        return remote(ref, ref, b2_ss.at[j, k - 1], b2_rs.at[j, k - 1], at_z(k))
 
     def ga(k):
-        ref = gw.at[(my_y + NY - k) % NY, :, my_c, :, lo]
+        ref = gw.at[y_of(k), :, my_c, lo]
         return remote(ref, ref, ga_ss.at[k], ga_rs.at[k], partner)
 
     def gb(k):
-        ref = gw.at[:, (my_z + NZ - k) % NZ, my_c, :, hi]
+        ref = gw.at[:, z_of(k), my_c, hi]
         return remote(ref, ref, gb_ss.at[k], gb_rs.at[k], partner)
 
-    def go_on(c):
-        c.start()
-        sent.append(c)
-
-    for k in (1, 2, 3):
+    far_y = (4, 3, 5, 2, 6, 1, 7)
+    far_z = (2, 1, 3)
+    for k in far_z:
         go_on(a1(k))
-    for k in (4, 3, 5, 2, 6, 1, 7):
+    for k in far_y:
         go_on(b1(k))
+    for k in far_y:
+        go_on(a2(0, k))
+    for k in far_z:
+        go_on(b2(0, k))
 
     for i in range(per):
         at = slice(i * heads, (i + 1) * heads)
@@ -295,33 +339,37 @@
         ns_out[i] = second[at]
         np_out[i] = plain[at]
 
-    for k in (1, 2, 3):
-        a1(k).wait_recv()
-    for k in (4, 3, 5, 2, 6, 1, 7):
-        go_on(a2(k))
-    for k in range(1, NY):
-        b1(k).wait_recv()
-    for k in (3, 2, 1):
-        go_on(b2(k))
+    for side, j in (("y", 1), ("y", 7), ("z", 1), ("z", 3), ("y", 2), ("y", 6), ("z", 2), ("y", 3), ("y", 5), ("y", 4)):
+        if side == "y":
+            b1(j).wait_recv()
+            for k in far_z:
+                go_on(b2(j, k))
+        else:
+            a1(j).wait_recv()
+            for k in far_y:
+                go_on(a2(j, k))
     go_on(ga(0))
     go_on(gb(0))
+
+    for side, k in (("y", 1), ("y", 7), ("z", 1), ("y", 2), ("y", 6), ("z", 3), ("y", 3), ("y", 5), ("z", 2), ("y", 4)):
+        if side == "y":
+            for j in range(NZ):
+                a2(j, k).wait_recv()
+            go_on(ga(k))
+        else:
+            for j in range(NY):
+                b2(j, k).wait_recv()
+            go_on(gb(k))
+    for k in range(NY):
+        ga(k).wait_recv()
+    for k in range(NZ):
+        gb(k).wait_recv()
 
     total = zh_send[my_h].astype(f32)
     for k in range(1, NH):
         h_copy(k).wait_recv()
         total = total + zh_recv[k - 1].astype(f32)
     gl_out[...] = total.astype(bf16)
-
-    for k in (1, 7, 2, 6, 3, 5, 4):
-        a2(k).wait_recv()
-        go_on(ga(k))
-    for k in (1, 2, 3):
-        b2(k).wait_recv()
-        go_on(gb(k))
-    for k in range(NY):
-        ga(k).wait_recv()
-    for k in range(NZ):
-        gb(k).wait_recv()
     for c in sent:
         c.wait_send()
 
@@ -342,7 +390,7 @@
         kernel,
         out_shape=(
             jax.ShapeDtypeStruct((share // NH, latw), bf16),
-            jax.ShapeDtypeStruct((NY, NZ, NC, per * heads, latw), bf16),
+            jax.ShapeDtypeStruct((NY, NZ, NC, per, heads, latw), bf16),
             jax.ShapeDtypeStruct((per, heads, latw), f32),
             jax.ShapeDtypeStruct((per, heads, latw), f32),
             jax.ShapeDtypeStruct((per, heads, latw), f32),
@@ -354,14 +402,19 @@
             V((heads, seq, rows), bf16),
             V((2, seq, seq), bf16),
             V((2, seq, seq), bf16),
-            V((heads, rows // 2, latw), f32),
-            V((heads, rows // 2, latw), bf16),
-            V((heads, rows // 2, latw), bf16),
-            V((heads, NY, 16, latw), bf16),
-            V((heads, NY - 1, 16, latw), bf16),
-            V((heads * 16, latw), bf16),
-            V((NZ, 16, latw), bf16),
-            V((NZ - 1, 16, latw), bf16),
+            V((heads, 2, rows // 2, latw // 2), f32),
+            V((heads, 2, rows // 2, latw // 2), bf16),
+            V((heads, 2, rows // 2, latw // 2), bf16),
+            V((heads, NY, 16, latw // 2), bf16),
+            V((heads, NY - 1, 16, latw // 2), bf16),
+            V((heads, NZ, 32, latw // 2), bf16),
+            V((heads, NZ - 1, 32, latw // 2), bf16),
+            V((heads * 16, latw // 2), bf16),
+            V((heads * 32, latw // 2), bf16),
+            V((NZ, 16, latw // 2), bf16),
+            V((NZ - 1, 16, latw // 2), bf16),
+            V((NY, 16, latw // 2), bf16),
+            V((NY - 1, 16, latw // 2), bf16),
             V((NX, share, latw), bf16),
             V((NX - 1, share, latw), bf16),
             V((NH, share // NH, latw), bf16),
@@ -373,13 +426,15 @@
             V((16, latw), f32),
             dma((heads,)), dma((heads,)),
             dma((heads, NY - 1)), dma((heads, NY - 1)),
+            dma((heads, NZ - 1)), dma((heads, NZ - 1)),
             dma((NZ - 1,)), dma((NZ - 1,)),
+            dma((NY - 1,)), dma((NY - 1,)),
             dma((NX - 1,)), dma((NX - 1,)),
             dma((NH - 1,)), dma((NH - 1,)),
             dma((NZ - 1,)), dma((NZ - 1,)),
             dma((NY - 1,)), dma((NY - 1,)),
-            dma((NY - 1,)), dma((NY - 1,)),
-            dma((NZ - 1,)), dma((NZ - 1,)),
+            dma((NZ, NY - 1)), dma((NZ, NY - 1)),
+            dma((NY, NZ - 1)), dma((NY, NZ - 1)),
             dma((NY,)), dma((NY,)),
             dma((NZ,)), dma((NZ,)),
         ],
@@ -387,7 +442,7 @@
             collective_id=0, has_side_effects=True, vmem_limit_bytes=60 * 2**20
         ),
     )(
-        offsets, latent, q_nope, q_rope, k_rope, grad_out, by_head, basis,
+        offsets, latent, q_nope, q_rope, k_rope.T, grad_out, by_head, basis,
         first_moment, second_rot, second_plain,
     )
     grad_latent, gathered, moment, rotated_sq, plain_sq = outs

time: 69.9 us -> 69.5 us (level)
    reshape x1 -> x0, local copies, waits for them, and re-layouts: 2.15 us -> none  [local(): gathered.reshape(rows, heads, latw)]
    unnamed x14 -> x12, local copies, waits for them, and re-layouts: 6.96 us -> 8.53 us
where the time goes in v2:
time: 69.5 us; the launch traced here: 69.1 us
  Pallas kernels  59.3 us (85%)
  local copies, waits for them, and re-layouts  8.53 us (12%)
  between operations  1.29 us (2%)
    pallas_call x1, Pallas kernels, local(): pl.pallas_call(kernel, out_shape=(jax.ShapeDtypeStruct((share // NH, latw...  59.3 us
    unnamed x12, local copies, waits for them, and re-layouts  8.53 us

profile of v2, /device:TPU:1, one launch (start us, length us, event | category | flops | bytes accessed | tf_op | source)
XLA Modules:
  0.0 69.1 jit_solution(10409140969463345635)
XLA Ops:
  1.3 2.4 %copy.18 = bf16[256,4,512]{2,0,1:T(8,128)(2,1)} copy(bf16[256,4,512]{2,1,0:T(4,128)(2,1)} %param.17) | data formatting | bytes 2097152 | tf_op args[6]
  3.7 59.3 %shard_map.146 = (bf16[48,512]{1,0:T(8,128)(2,1)}, bf16[8,4,2,4,4,512]{5,4,3,2,1,0:T(4,128)(2,1)}, f32[4,4,512]{2,1,0:T(4,128)}, f32[4,4,512]{2,1,0:T(4,128)}, f32[4,4,512]{2,1,0:T(4,128)}) custom-call(s32[1]{0:T(128)S(6)} %copy.24.off, bf16[576,512]{1,0:T(8,128)(2,1)} %lat.1, bf16[576,512]{1,0:T(8,128)(2,1)} %qn.1, bf16[576,256]{1,0:T(8,128)(2,1)} %qr.1, ...), custom_call_target="tpu_custom_call" | custom-call | tf_op jit(solution)/shard_map/pallas_call | solution.py:389
  63.0 1.4 %copy.25 = bf16[48,512]{1,0:T(8,128)(2,1)} copy(bf16[48,512]{1,0:T(8,128)(2,1)} %get-tuple-element.20) | data formatting | bytes 98304
  64.4 0.0 copy-start.2
  64.4 2.6 %copy.26 = bf16[256,4,512]{2,1,0:T(4,128)(2,1)} copy(bf16[256,4,512]{2,1,0:T(4,128)(2,1)} %bitcast.6) | data formatting | bytes 2097152
  67.0 0.0 copy-done.2
  67.0 0.0 copy-start.1
  67.0 0.6 copy.27
  67.6 0.2 copy-done.1
  67.7 0.0 copy-start
  67.7 0.6 copy.28
  68.3 0.2 copy-done
  68.5 0.6 copy.29
Async XLA Ops:
  64.4 2.6 %copy-start.2 = (f32[4,4,512]{2,1,0:T(4,128)S(1)}, f32[4,4,512]{2,1,0:T(4,128)}, u32[]{:S(2)}) copy-start(f32[4,4,512]{2,1,0:T(4,128)} %get-tuple-element.22) | copy-start | bytes 98308
  67.0 0.8 %copy-start.1 = (f32[4,4,512]{2,1,0:T(4,128)S(1)}, f32[4,4,512]{2,1,0:T(4,128)}, u32[]{:S(2)}) copy-start(f32[4,4,512]{2,1,0:T(4,128)} %get-tuple-element.23) | copy-start | bytes 98308
  67.7 0.8 %copy-start = (f32[4,4,512]{2,1,0:T(4,128)S(1)}, f32[4,4,512]{2,1,0:T(4,128)}, u32[]{:S(2)}) copy-start(f32[4,4,512]{2,1,0:T(4,128)} %get-tuple-element.24) | copy-start | bytes 98308

commit v3 on v2

--- a/solution.py
+++ b/solution.py
@@ -43,14 +43,26 @@
 
 
 def kernel(
-    off, lat, qn, qr, kr, go, w, basis, fm, sr, sp,
+    off, lat_in, qn_in, qr_in, kr_in, go_in, w_in, basis_in, fm_in, sr_in, sp_in,
     gl_out, gw, nf_out, ns_out, np_out,
-    krp, gkv, pts, gss, wg_own, wg_send, c_recv, y_send, y_recv, z_send, z_recv,
+    lat, w_raw, kr, qn, qr, go, basis, fm, sr, sp, in_sem, w, krp, gkv, pts, gss, wg_own, wg_send, c_recv, y_send, y_recv, z_send, z_recv,
     asrc, bsrc, za_send, za_recv, yb_send, yb_recv,
-    gl_send, x_recv, zh_send, zh_recv, b_hi, b_lo, t_fm, t_sr, t_sp,
-    c_ss, c_rs, y_ss, y_rs, z_ss, z_rs, za_ss, za_rs, yb_ss, yb_rs, x_ss, x_rs, h_ss, h_rs,
+    gl_send, x1_recv, x2_send, x2_recv, zh_send, zh_recv, b_hi, b_lo, t_fm, t_sr, t_sp,
+    c_ss, c_rs, y_ss, y_rs, z_ss, z_rs, za_ss, za_rs, yb_ss, yb_rs, x1_ss, x1_rs, x2_ss, x2_rs, h_ss, h_rs,
     a1_ss, a1_rs, b1_ss, b1_rs, a2_ss, a2_rs, b2_ss, b2_rs, ga_ss, ga_rs, gb_ss, gb_rs,
 ):
+    loads = {
+        name: pltpu.make_async_copy(src, dst, in_sem.at[i])
+        for i, (name, src, dst) in enumerate(
+            (
+                ("lat", lat_in, lat), ("w", w_in, w_raw), ("kr", kr_in, kr), ("qn", qn_in, qn),
+                ("qr", qr_in, qr), ("go", go_in, go), ("basis", basis_in, basis),
+                ("fm", fm_in, fm), ("sr", sr_in, sr), ("sp", sp_in, sp),
+            )
+        )
+    }
+    for load in loads.values():
+        load.start()
     seq, _ = lat.shape
     heads, rows, latw = w.shape
     hd = rows // 2
@@ -66,8 +78,12 @@
     def at_z(k):
         return (my_y * (NZ * NC) + ((my_z + k) % NZ) * NC + my_c, tn)
 
-    def at_x(k):
-        return (dp, ((my_x + k) % NX) * NH + my_h)
+    x_near = my_x + 1 - 2 * (my_x % 2)
+    x_far = NX - 1 - my_x
+    x_to = ((x_near, NX - 1 - x_near), (x_far, x_far + 1 - 2 * (x_far % 2)))
+
+    def at_x(x):
+        return (dp, x * NH + my_h)
 
     def at_h(k):
         return (dp, my_x * NH + (my_h + k) % NH)
@@ -85,7 +101,7 @@
         [partner]
         + [at_y(k) for k in range(1, NY)]
         + [at_z(k) for k in range(1, NZ)]
-        + [at_x(k) for k in range(1, NX)]
+        + [at_x(x_near), at_x(x_far)]
         + [at_h(k) for k in range(1, NH)]
     )
     for to in greet:
@@ -93,6 +109,7 @@
 
     sent = []
 
+    loads["kr"].wait()
     rope = kr.shape[0]
     lane = iota((rope, 2 * rope), 1)
     row = iota((rope, 2 * rope), 0)
@@ -140,6 +157,9 @@
         for k in (2, 1, 3):
             go_on(z_copy(h, k))
 
+    loads["lat"].wait()
+    loads["w"].wait()
+    w[...] = pltpu.einshape("rhc->hrc", w_raw[...])
     for h in range(heads):
         lanes = slice(h * hd, (h + 1) * hd)
         pair = slice((h // 2) * hd, (h // 2 + 1) * hd)
@@ -147,6 +167,9 @@
         key = jnp.concatenate([kv[:, :hd], krp[h % 2]], axis=1)
         value = kv[:, hd:]
         buf = h % 2
+        if h == 0:
+            for name in ("qn", "qr", "go"):
+                loads[name].wait()
         for start, size in blocks:
             at = slice(start, start + size)
             query = jnp.concatenate([qn[at, lanes], qr[at, pair]], axis=1)
@@ -185,20 +208,34 @@
         total = mm(gkv[0, at], w[0])
         for h in range(1, heads):
             total = total + mm(gkv[h, at], w[h])
-        gl_send[xb] = total.astype(bf16)
+        gl_send[0, xb] = total[:, :half].astype(bf16)
+        gl_send[1, xb] = total[:, half:].astype(bf16)
+
+    def x1_copy(side, slot):
+        return remote(
+            gl_send.at[side, x_to[side][slot]], x1_recv.at[side, slot],
+            x1_ss.at[side, slot], x1_rs.at[side, slot], at_x(x_to[side][0]),
+        )
+
+    def x2_copy(side):
+        return remote(
+            x2_send.at[side], x2_recv.at[side], x2_ss.at[side], x2_rs.at[side], at_x(x_to[1 - side][0])
+        )
+
+    for slot in (1, 0):
+        for side in range(2):
+            go_on(x1_copy(side, slot))
 
     finish_core(heads - 1)
 
-    def x_copy(k):
-        return remote(
-            gl_send.at[(my_x + k) % NX], x_recv.at[k - 1], x_ss.at[k - 1], x_rs.at[k - 1], at_x(k)
-        )
-
-    for k in (2, 1, 3):
-        c = x_copy(k)
-        c.start()
-        sent.append(c)
-
+    for side in range(2):
+        x1_copy(side, 1).wait_recv()
+        total = gl_send[side, x_to[1 - side][0]].astype(f32) + x1_recv[side, 1].astype(f32)
+        x2_send[side] = total.astype(bf16)
+        go_on(x2_copy(side))
+
+    for name in ("basis", "fm", "sr", "sp"):
+        loads[name].wait()
     high, low = split(basis[...])
     b_hi[...] = high
     b_lo[...] = low
@@ -251,11 +288,15 @@
     for k in (2, 1, 3):
         go_on(za_copy(k))
 
-    total = gl_send[my_x].astype(f32)
-    for k in range(1, NX):
-        x_copy(k).wait_recv()
-        total = total + x_recv[k - 1].astype(f32)
-    zh_send[...] = total.astype(bf16).reshape(NH, share // NH, latw)
+    for side in range(2):
+        x1_copy(side, 0).wait_recv()
+        x2_copy(side).wait_recv()
+        total = (
+            gl_send[side, my_x].astype(f32) + x1_recv[side, 0].astype(f32) + x2_recv[side].astype(f32)
+        )
+        zh_send[:, :, side * half : (side + 1) * half] = total.astype(bf16).reshape(
+            NH, share // NH, half
+        )
 
     def h_copy(k):
         return remote(
@@ -374,6 +415,33 @@
         c.wait_send()
 
 
+def hand_over(*refs):
+    n = (len(refs) - 2) // 3
+    ins, outs, held, in_sem, out_sem = refs[:n], refs[n : 2 * n], refs[2 * n : 3 * n], *refs[3 * n :]
+    loads = [pltpu.make_async_copy(ins[i], held[i], in_sem.at[i]) for i in range(n)]
+    stores = [pltpu.make_async_copy(held[i], outs[i], out_sem.at[i]) for i in range(n)]
+    for i in range(n):
+        loads[i].start()
+    for i in range(n):
+        loads[i].wait()
+        stores[i].start()
+    for i in range(n):
+        stores[i].wait()
+
+
+def store(*arrays):
+    anywhere = pl.BlockSpec(memory_space=pl.ANY)
+    sem = pltpu.SemaphoreType.DMA((len(arrays),))
+    return pl.pallas_call(
+        hand_over,
+        out_shape=[jax.ShapeDtypeStruct(a.shape, a.dtype) for a in arrays],
+        in_specs=[anywhere] * len(arrays),
+        out_specs=[anywhere] * len(arrays),
+        scratch_shapes=[pltpu.VMEM(a.shape, a.dtype) for a in arrays] + [sem, sem],
+        compiler_params=pltpu.CompilerParams(vmem_limit_bytes=60 * 2**20),
+    )(*arrays)
+
+
 def local(
     latent, q_nope, q_rope, k_rope, grad_out, offsets, weight, basis,
     first_moment, second_rot, second_plain,
@@ -381,8 +449,8 @@
     seq, latw = latent.shape
     rows, heads, _ = weight.shape
     per = first_moment.shape[0]
-    by_head = jnp.transpose(weight, (1, 0, 2))
     vmem = pl.BlockSpec(memory_space=pltpu.VMEM)
+    anywhere = pl.BlockSpec(memory_space=pl.ANY)
     dma = pltpu.SemaphoreType.DMA
     V = pltpu.VMEM
     share = seq // NX
@@ -395,9 +463,13 @@
             jax.ShapeDtypeStruct((per, heads, latw), f32),
             jax.ShapeDtypeStruct((per, heads, latw), f32),
         ),
-        in_specs=[pl.BlockSpec(memory_space=pltpu.SMEM)] + [vmem] * 10,
+        in_specs=[pl.BlockSpec(memory_space=pltpu.SMEM)] + [anywhere] * 10,
         out_specs=[vmem] * 5,
         scratch_shapes=[
+            V(latent.shape, bf16), V(weight.shape, bf16), V(k_rope.shape[::-1], bf16),
+            V(q_nope.shape, bf16), V(q_rope.shape, bf16), V(grad_out.shape, bf16),
+            V(basis.shape, f32), V(first_moment.shape, f32), V(first_moment.shape, f32),
+            V(first_moment.shape, f32), dma((10,)), V((heads, rows, latw), bf16),
             V((2, seq, 128), bf16),
             V((heads, seq, rows), bf16),
             V((2, seq, seq), bf16),
@@ -415,8 +487,10 @@
             V((NZ - 1, 16, latw // 2), bf16),
             V((NY, 16, latw // 2), bf16),
             V((NY - 1, 16, latw // 2), bf16),
-            V((NX, share, latw), bf16),
-            V((NX - 1, share, latw), bf16),
+            V((2, NX, share, latw // 2), bf16),
+            V((2, 2, share, latw // 2), bf16),
+            V((2, share, latw // 2), bf16),
+            V((2, share, latw // 2), bf16),
             V((NH, share // NH, latw), bf16),
             V((NH - 1, share // NH, latw), bf16),
             V((latw, latw), bf16),
@@ -429,7 +503,8 @@
             dma((heads, NZ - 1)), dma((heads, NZ - 1)),
             dma((NZ - 1,)), dma((NZ - 1,)),
             dma((NY - 1,)), dma((NY - 1,)),
-            dma((NX - 1,)), dma((NX - 1,)),
+            dma((2, 2)), dma((2, 2)),
+            dma((2,)), dma((2,)),
             dma((NH - 1,)), dma((NH - 1,)),
             dma((NZ - 1,)), dma((NZ - 1,)),
             dma((NY - 1,)), dma((NY - 1,)),
@@ -442,11 +517,10 @@
             collective_id=0, has_side_effects=True, vmem_limit_bytes=60 * 2**20
         ),
     )(
-        offsets, latent, q_nope, q_rope, k_rope.T, grad_out, by_head, basis,
+        offsets, latent, q_nope, q_rope, k_rope.T, grad_out, weight, basis,
         first_moment, second_rot, second_plain,
     )
-    grad_latent, gathered, moment, rotated_sq, plain_sq = outs
-    return (grad_latent, gathered.reshape(rows, heads, latw), moment, rotated_sq, plain_sq)
+    return store(outs[0], outs[1].reshape(rows, heads, latw), *outs[2:])
 
 
 def solution(mesh):

time: 69.5 us -> 58.3 us (0.84)
  local copies, waits for them, and re-layouts: 8.53 us -> 0 us
  Pallas kernels: 59.3 us -> 56.9 us
    unnamed x12 -> x0, local copies, waits for them, and re-layouts: 8.53 us -> none
    pallas_call x1, Pallas kernels: 59.3 us -> 54.5 us  [local(): pl.pallas_call(kernel, out_shape=(jax.ShapeDtypeStruct((share // NH, latw...]
    pallas_call x0 -> x1, Pallas kernels: none -> 2.32 us  [store(): pl.pallas_call(hand_over, out_shape=[jax.ShapeDtypeStruct(a.shape, a.dtyp...]
where the time goes in v3:
time: 58.3 us; the launch traced here: 58.1 us
  Pallas kernels  56.9 us (98%)
  between operations  1.29 us (2%)
    pallas_call x1, Pallas kernels, local(): pl.pallas_call(kernel, out_shape=(jax.ShapeDtypeStruct((share // NH, latw...  54.5 us
    pallas_call x1, Pallas kernels, store(): pl.pallas_call(hand_over, out_shape=[jax.ShapeDtypeStruct(a.shape, a.dtyp...  2.32 us

profile of v3, /device:TPU:1, one launch (start us, length us, event | category | flops | bytes accessed | tf_op | source)
XLA Modules:
  0.0 58.1 jit_solution(7420169501075048948)
XLA Ops:
  1.3 54.5 %shard_map.146 = (bf16[48,512]{1,0:T(8,128)(2,1)}, bf16[8,4,2,4,4,512]{5,4,3,2,1,0:T(4,128)(2,1)}, f32[4,4,512]{2,1,0:T(4,128)}, f32[4,4,512]{2,1,0:T(4,128)}, f32[4,4,512]{2,1,0:T(4,128)}) custom-call(s32[1]{0:T(128)S(6)} %copy.16.off, bf16[576,512]{1,0:T(8,128)(2,1)} %lat_in.1, bf16[576,512]{1,0:T(8,128)(2,1)} %qn_in.1, bf16[576,256]{1,0:T(8,128)(2,1)} %qr_in.1, ...), custom_call_target="tpu_custom_call" | custom-call | tf_op jit(solution)/shard_map/pallas_call | solution.py:457
  55.8 2.3 %shard_map.147 = (bf16[48,512]{1,0:T(8,128)(2,1)}, bf16[256,4,512]{2,1,0:T(4,128)(2,1)}, f32[4,4,512]{2,1,0:T(4,128)}, f32[4,4,512]{2,1,0:T(4,128)}, f32[4,4,512]{2,1,0:T(4,128)}) custom-call(bf16[48,512]{1,0:T(8,128)(2,1)} %get-tuple-element.10.refs_0_, bf16[256,4,512]{2,1,0:T(4,128)(2,1)} %bitcast.2, f32[4,4,512]{2,1,0:T(4,128)} %get-tuple-element.12.refs_2_, ...), custom_call_target="tpu_custom_call" | custom-call | tf_op jit(solution)/shard_map/pallas_call | solution.py:435

commit v4 on v3

--- a/solution.py
+++ b/solution.py
@@ -125,7 +125,7 @@
     scale = float(hd + rope) ** (-0.5)
     to_exp2 = scale * math.log2(math.e)
     last_seen = off[0] - 1
-    blocks = [(0, 256), (256, 256), (512, seq - 512)]
+    blocks = [(512, seq - 512), (0, 256), (256, 256)]
 
     def core_copy(h):
         return remote(wg_send.at[h], c_recv.at[h], c_ss.at[h], c_rs.at[h], partner)
@@ -160,32 +160,42 @@
     loads["lat"].wait()
     loads["w"].wait()
     w[...] = pltpu.einshape("rhc->hrc", w_raw[...])
-    for h in range(heads):
+    def front(h, start, size, key, value):
         lanes = slice(h * hd, (h + 1) * hd)
-        pair = slice((h // 2) * hd, (h // 2 + 1) * hd)
+        at = slice(start, start + size)
+        query = jnp.concatenate([qn[at, lanes], qr[at, (h // 2) * hd : (h // 2 + 1) * hd]], axis=1)
+        return mm(key, query, NT), mm(value, go[at, lanes], NT)
+
+    def open_head(h):
         kv = mm(lat[...], w[h], NT).astype(bf16)
-        key = jnp.concatenate([kv[:, :hd], krp[h % 2]], axis=1)
-        value = kv[:, hd:]
+        return jnp.concatenate([kv[:, :hd], krp[h % 2]], axis=1), kv[:, hd:]
+
+    steps = [(h, start, size) for h in range(heads) for start, size in blocks]
+    key, value = open_head(0)
+    for name in ("qn", "qr", "go"):
+        loads[name].wait()
+    ahead = front(*steps[0], key, value)
+    for n, (h, start, size) in enumerate(steps):
+        lanes = slice(h * hd, (h + 1) * hd)
         buf = h % 2
-        if h == 0:
-            for name in ("qn", "qr", "go"):
-                loads[name].wait()
-        for start, size in blocks:
-            at = slice(start, start + size)
-            query = jnp.concatenate([qn[at, lanes], qr[at, pair]], axis=1)
-            scores = mm(key, query, NT)
-            limit = jnp.maximum(iota((1, size), 1) + start, last_seen)
-            seen = iota((seq, size), 0) <= limit
-            masked = jnp.where(seen, scores, -jnp.inf)
-            top = jnp.max(masked, axis=0, keepdims=True)
-            terms = jnp.exp2((masked - top) * to_exp2)
-            probs = terms * (1.0 / jnp.sum(terms, axis=0, keepdims=True))
-            low = probs.astype(bf16)
-            pts[buf, :, at] = low
-            grad_probs = mm(value, go[at, lanes], NT)
-            delta = jnp.sum(low.astype(f32) * grad_probs, axis=0, keepdims=True)
-            gss[buf, :, at] = (probs * (grad_probs - delta) * scale).astype(bf16)
-        grad_keys = mm(gss[buf], qn[:, lanes])
+        scores, grad_probs = ahead
+        if n + 1 < len(steps):
+            if steps[n + 1][0] != h:
+                key, value = open_head(h + 1)
+            ahead = front(*steps[n + 1], key, value)
+        limit = jnp.maximum(iota((1, size), 1) + start, last_seen)
+        seen = iota((seq, size), 0) <= limit
+        masked = jnp.where(seen, scores, -jnp.inf)
+        top = jnp.max(masked, axis=0, keepdims=True)
+        terms = jnp.exp2((masked - top) * to_exp2)
+        low = (terms * (1.0 / jnp.sum(terms, axis=0, keepdims=True))).astype(bf16)
+        wide = low.astype(f32)
+        delta = jnp.sum(wide * grad_probs, axis=0, keepdims=True)
+        pts[buf, :, start : start + size] = low
+        gss[buf, :, start : start + size] = (wide * (grad_probs - delta)).astype(bf16)
+        if (start, size) != blocks[-1]:
+            continue
+        grad_keys = mm(gss[buf], qn[:, lanes]) * scale
         grad_values = mm(pts[buf], go[:, lanes])
         both = jnp.concatenate([grad_keys.astype(bf16), grad_values.astype(bf16)], axis=1)
         gkv[h] = both
@@ -416,30 +426,22 @@
 
 
 def hand_over(*refs):
-    n = (len(refs) - 2) // 3
-    ins, outs, held, in_sem, out_sem = refs[:n], refs[n : 2 * n], refs[2 * n : 3 * n], *refs[3 * n :]
-    loads = [pltpu.make_async_copy(ins[i], held[i], in_sem.at[i]) for i in range(n)]
-    stores = [pltpu.make_async_copy(held[i], outs[i], out_sem.at[i]) for i in range(n)]
-    for i in range(n):
-        loads[i].start()
-    for i in range(n):
-        loads[i].wait()
-        stores[i].start()
-    for i in range(n):
-        stores[i].wait()
+    n = (len(refs) - 1) // 2
+    stores = [pltpu.make_async_copy(refs[i], refs[n + i], refs[-1].at[i]) for i in range(n)]
+    for copy in stores:
+        copy.start()
+    for copy in stores:
+        copy.wait()
 
 
 def store(*arrays):
-    anywhere = pl.BlockSpec(memory_space=pl.ANY)
-    sem = pltpu.SemaphoreType.DMA((len(arrays),))
     return pl.pallas_call(
         hand_over,
         out_shape=[jax.ShapeDtypeStruct(a.shape, a.dtype) for a in arrays],
-        in_specs=[anywhere] * len(arrays),
-        out_specs=[anywhere] * len(arrays),
-        scratch_shapes=[pltpu.VMEM(a.shape, a.dtype) for a in arrays] + [sem, sem],
-        compiler_params=pltpu.CompilerParams(vmem_limit_bytes=60 * 2**20),
-    )(*arrays)
+        in_specs=[pl.BlockSpec(memory_space=pltpu.VMEM)] * len(arrays),
+        out_specs=[pl.BlockSpec(memory_space=pl.ANY)] * len(arrays),
+        scratch_shapes=[pltpu.SemaphoreType.DMA((len(arrays),))],
+    )(*(pltpu.with_memory_space_constraint(a, pltpu.VMEM) for a in arrays))
 
 
 def local(
@@ -457,11 +459,11 @@
     outs = pl.pallas_call(
         kernel,
         out_shape=(
-            jax.ShapeDtypeStruct((share // NH, latw), bf16),
-            jax.ShapeDtypeStruct((NY, NZ, NC, per, heads, latw), bf16),
-            jax.ShapeDtypeStruct((per, heads, latw), f32),
-            jax.ShapeDtypeStruct((per, heads, latw), f32),
-            jax.ShapeDtypeStruct((per, heads, latw), f32),
+            V((share // NH, latw), bf16),
+            V((NY, NZ, NC, per, heads, latw), bf16),
+            V((per, heads, latw), f32),
+            V((per, heads, latw), f32),
+            V((per, heads, latw), f32),
         ),
         in_specs=[pl.BlockSpec(memory_space=pltpu.SMEM)] + [anywhere] * 10,
         out_specs=[vmem] * 5,
@@ -520,7 +522,8 @@
         offsets, latent, q_nope, q_rope, k_rope.T, grad_out, weight, basis,
         first_moment, second_rot, second_plain,
     )
-    return store(outs[0], outs[1].reshape(rows, heads, latw), *outs[2:])
+    outs = store(*outs)
+    return (outs[0], outs[1].reshape(rows, heads, latw), *outs[2:])
 
 
 def solution(mesh):

time: 58.3 us -> 54.8 us (0.940)
  Pallas kernels: 56.9 us -> 53.4 us
    pallas_call x1, Pallas kernels: 54.5 us -> 52.3 us  [local(): pl.pallas_call(kernel, out_shape=(V((share // NH, latw), bf16), V((NY, NZ...]
    pallas_call x1, Pallas kernels: 2.32 us -> 1.04 us  [store(): pl.pallas_call(hand_over, out_shape=[jax.ShapeDtypeStruct(a.shape, a.dtyp...]
where the time goes in v4:
time: 54.8 us; the launch traced here: 54.7 us
  Pallas kernels  53.4 us (97%)
  between operations  1.29 us (2%)
    pallas_call x1, Pallas kernels, local(): pl.pallas_call(kernel, out_shape=(V((share // NH, latw), bf16), V((NY, NZ...  52.3 us

profile of v4, /device:TPU:1, one launch (start us, length us, event | category | flops | bytes accessed | tf_op | source)
XLA Modules:
  0.0 54.7 jit_solution(11857547336943213992)
XLA Ops:
  1.3 52.3 %shard_map.146 = (bf16[48,512]{1,0:T(8,128)(2,1)S(1)}, bf16[8,4,2,4,4,512]{5,4,3,2,1,0:T(4,128)(2,1)S(1)}, f32[4,4,512]{2,1,0:T(4,128)S(1)}, f32[4,4,512]{2,1,0:T(4,128)S(1)}, f32[4,4,512]{2,1,0:T(4,128)S(1)}) custom-call(s32[1]{0:T(128)S(6)} %copy.16.off, bf16[576,512]{1,0:T(8,128)(2,1)} %lat_in.1, bf16[576,512]{1,0:T(8,128)(2,1)} %qn_in.1, ...), custom_call_target="tpu_custom_call" | custom-call | tf_op jit(solution)/shard_map/pallas_call | solution.py:459
  53.6 1.0 %shard_map.147 = (bf16[48,512]{1,0:T(8,128)(2,1)}, bf16[8,4,2,4,4,512]{5,4,3,2,1,0:T(4,128)(2,1)}, f32[4,4,512]{2,1,0:T(4,128)}, f32[4,4,512]{2,1,0:T(4,128)}, f32[4,4,512]{2,1,0:T(4,128)}) custom-call(bf16[48,512]{1,0:T(8,128)(2,1)S(1)} %get-tuple-element.15.refs_0_, bf16[8,4,2,4,4,512]{5,4,3,2,1,0:T(4,128)(2,1)S(1)} %get-tuple-element.16.refs_1_, ...), custom_call_target="tpu_custom_call" | custom-call | tf_op jit(solution)/shard_map/pallas_call | solution.py:438

commit v5 on v4

--- a/solution.py
+++ b/solution.py
@@ -61,8 +61,10 @@
             )
         )
     }
-    for load in loads.values():
-        load.start()
+    late = ("basis", "fm", "sr", "sp")
+    for name, load in loads.items():
+        if name not in late:
+            load.start()
     seq, _ = lat.shape
     heads, rows, latw = w.shape
     hd = rows // 2
@@ -174,6 +176,8 @@
     key, value = open_head(0)
     for name in ("qn", "qr", "go"):
         loads[name].wait()
+    for name in late:
+        loads[name].start()
     ahead = front(*steps[0], key, value)
     for n, (h, start, size) in enumerate(steps):
         lanes = slice(h * hd, (h + 1) * hd)
@@ -193,6 +197,8 @@
         delta = jnp.sum(wide * grad_probs, axis=0, keepdims=True)
         pts[buf, :, start : start + size] = low
         gss[buf, :, start : start + size] = (wide * (grad_probs - delta)).astype(bf16)
+        if (start, size) == blocks[1] and h > 0:
+            finish_core(h - 1)
         if (start, size) != blocks[-1]:
             continue
         grad_keys = mm(gss[buf], qn[:, lanes]) * scale
@@ -209,8 +215,6 @@
         c = core_copy(h)
         c.start()
         sent.append(c)
-        if h > 0:
-            finish_core(h - 1)
 
     share = seq // NX
     for xb in range(NX):
@@ -244,7 +248,7 @@
         x2_send[side] = total.astype(bf16)
         go_on(x2_copy(side))
 
-    for name in ("basis", "fm", "sr", "sp"):
+    for name in late:
         loads[name].wait()
     high, low = split(basis[...])
     b_hi[...] = high
@@ -353,13 +357,18 @@
         ref = gw.at[my_y, my_z, my_c, lo]
         return remote(ref, ref, a1_ss.at[k - 1], a1_rs.at[k - 1], at_z(k))
 
+    def along_y(k):
+        return (y_of(5), at_y(NY - 1)) if k == 4 else (my_y, at_y(k))
+
     def b1(k):
-        ref = gw.at[my_y, my_z, my_c, hi]
-        return remote(ref, ref, b1_ss.at[k - 1], b1_rs.at[k - 1], at_y(k))
+        row, to = along_y(k)
+        ref = gw.at[row, my_z, my_c, hi]
+        return remote(ref, ref, b1_ss.at[k - 1], b1_rs.at[k - 1], to)
 
     def a2(j, k):
-        ref = gw.at[my_y, z_of(j), my_c, lo]
-        return remote(ref, ref, a2_ss.at[j, k - 1], a2_rs.at[j, k - 1], at_y(k))
+        row, to = along_y(k)
+        ref = gw.at[row, z_of(j), my_c, lo]
+        return remote(ref, ref, a2_ss.at[j, k - 1], a2_rs.at[j, k - 1], to)
 
     def b2(j, k):
         ref = gw.at[y_of(j), my_z, my_c, hi]
@@ -373,7 +382,7 @@
         ref = gw.at[:, z_of(k), my_c, hi]
         return remote(ref, ref, gb_ss.at[k], gb_rs.at[k], partner)
 
-    far_y = (4, 3, 5, 2, 6, 1, 7)
+    far_y = (5, 3, 6, 2, 7, 1)
     far_z = (2, 1, 3)
     for k in far_z:
         go_on(a1(k))
@@ -390,9 +399,11 @@
         ns_out[i] = second[at]
         np_out[i] = plain[at]
 
-    for side, j in (("y", 1), ("y", 7), ("z", 1), ("z", 3), ("y", 2), ("y", 6), ("z", 2), ("y", 3), ("y", 5), ("y", 4)):
+    for side, j in (("y", 1), ("y", 7), ("z", 1), ("z", 3), ("y", 5), ("y", 2), ("y", 6), ("z", 2), ("y", 3), ("y", 4)):
         if side == "y":
             b1(j).wait_recv()
+            if j == 5:
+                go_on(b1(4))
             for k in far_z:
                 go_on(b2(j, k))
         else:
@@ -402,10 +413,12 @@
     go_on(ga(0))
     go_on(gb(0))
 
-    for side, k in (("y", 1), ("y", 7), ("z", 1), ("y", 2), ("y", 6), ("z", 3), ("y", 3), ("y", 5), ("z", 2), ("y", 4)):
+    for side, k in (("y", 5), ("y", 1), ("y", 7), ("z", 1), ("y", 2), ("y", 6), ("z", 3), ("y", 3), ("z", 2), ("y", 4)):
         if side == "y":
             for j in range(NZ):
                 a2(j, k).wait_recv()
+                if k == 5:
+                    go_on(a2(j, 4))
             go_on(ga(k))
         else:
             for j in range(NY):

time: 54.8 us -> 57.6 us (1.051)
  Pallas kernels: 53.4 us -> 56.2 us
    pallas_call x1, Pallas kernels: 52.3 us -> 55.2 us  [local(): pl.pallas_call(kernel, out_shape=(V((share // NH, latw), bf16), V((NY, NZ...]
where the time goes in v5:
time: 57.6 us; the launch traced here: 57.5 us
  Pallas kernels  56.2 us (98%)
  between operations  1.29 us (2%)
    pallas_call x1, Pallas kernels, local(): pl.pallas_call(kernel, out_shape=(V((share // NH, latw), bf16), V((NY, NZ...  55.2 us

profile of v5, /device:TPU:1, one launch (start us, length us, event | category | flops | bytes accessed | tf_op | source)
XLA Modules:
  0.0 57.5 jit_solution(13575688443233702835)
XLA Ops:
  1.3 55.2 %shard_map.146 = (bf16[48,512]{1,0:T(8,128)(2,1)S(1)}, bf16[8,4,2,4,4,512]{5,4,3,2,1,0:T(4,128)(2,1)S(1)}, f32[4,4,512]{2,1,0:T(4,128)S(1)}, f32[4,4,512]{2,1,0:T(4,128)S(1)}, f32[4,4,512]{2,1,0:T(4,128)S(1)}) custom-call(s32[1]{0:T(128)S(6)} %copy.16.off, bf16[576,512]{1,0:T(8,128)(2,1)} %lat_in.1, bf16[576,512]{1,0:T(8,128)(2,1)} %qn_in.1, ...), custom_call_target="tpu_custom_call" | custom-call | tf_op jit(solution)/shard_map/pallas_call | solution.py:472
  56.4 1.0 %shard_map.147 = (bf16[48,512]{1,0:T(8,128)(2,1)}, bf16[8,4,2,4,4,512]{5,4,3,2,1,0:T(4,128)(2,1)}, f32[4,4,512]{2,1,0:T(4,128)}, f32[4,4,512]{2,1,0:T(4,128)}, f32[4,4,512]{2,1,0:T(4,128)}) custom-call(bf16[48,512]{1,0:T(8,128)(2,1)S(1)} %get-tuple-element.15.refs_0_, bf16[8,4,2,4,4,512]{5,4,3,2,1,0:T(4,128)(2,1)S(1)} %get-tuple-element.16.refs_1_, ...), custom_call_target="tpu_custom_call" | custom-call | tf_op jit(solution)/shard_map/pallas_call | solution.py:451

commit v6 on v4

--- a/solution.py
+++ b/solution.py
@@ -61,8 +61,10 @@
             )
         )
     }
-    for load in loads.values():
-        load.start()
+    late = ("basis", "fm", "sr", "sp")
+    for name, load in loads.items():
+        if name not in late:
+            load.start()
     seq, _ = lat.shape
     heads, rows, latw = w.shape
     hd = rows // 2
@@ -174,6 +176,8 @@
     key, value = open_head(0)
     for name in ("qn", "qr", "go"):
         loads[name].wait()
+    for name in late:
+        loads[name].start()
     ahead = front(*steps[0], key, value)
     for n, (h, start, size) in enumerate(steps):
         lanes = slice(h * hd, (h + 1) * hd)
@@ -244,7 +248,7 @@
         x2_send[side] = total.astype(bf16)
         go_on(x2_copy(side))
 
-    for name in ("basis", "fm", "sr", "sp"):
+    for name in late:
         loads[name].wait()
     high, low = split(basis[...])
     b_hi[...] = high

time: 54.8 us -> 54.9 us (level)
  no operation moved by 1% of the time
where the time goes in v6:
time: 54.9 us; the launch traced here: 54.8 us
  Pallas kernels  53.5 us (97%)
  between operations  1.29 us (2%)
    pallas_call x1, Pallas kernels, local(): pl.pallas_call(kernel, out_shape=(V((share // NH, latw), bf16), V((NY, NZ...  52.5 us

profile of v6, /device:TPU:1, one launch (start us, length us, event | category | flops | bytes accessed | tf_op | source)
XLA Modules:
  0.0 54.8 jit_solution(13571187071760548218)
XLA Ops:
  1.3 52.5 %shard_map.146 = (bf16[48,512]{1,0:T(8,128)(2,1)S(1)}, bf16[8,4,2,4,4,512]{5,4,3,2,1,0:T(4,128)(2,1)S(1)}, f32[4,4,512]{2,1,0:T(4,128)S(1)}, f32[4,4,512]{2,1,0:T(4,128)S(1)}, f32[4,4,512]{2,1,0:T(4,128)S(1)}) custom-call(s32[1]{0:T(128)S(6)} %copy.16.off, bf16[576,512]{1,0:T(8,128)(2,1)} %lat_in.1, bf16[576,512]{1,0:T(8,128)(2,1)} %qn_in.1, ...), custom_call_target="tpu_custom_call" | custom-call | tf_op jit(solution)/shard_map/pallas_call | solution.py:463
  53.7 1.0 %shard_map.147 = (bf16[48,512]{1,0:T(8,128)(2,1)}, bf16[8,4,2,4,4,512]{5,4,3,2,1,0:T(4,128)(2,1)}, f32[4,4,512]{2,1,0:T(4,128)}, f32[4,4,512]{2,1,0:T(4,128)}, f32[4,4,512]{2,1,0:T(4,128)}) custom-call(bf16[48,512]{1,0:T(8,128)(2,1)S(1)} %get-tuple-element.15.refs_0_, bf16[8,4,2,4,4,512]{5,4,3,2,1,0:T(4,128)(2,1)S(1)} %get-tuple-element.16.refs_1_, ...), custom_call_target="tpu_custom_call" | custom-call | tf_op jit(solution)/shard_map/pallas_call | solution.py:442
